TPU v7x, 32 devices: a whole 2x2x4 slice. The times are simulated.
32 devices in a mesh: groups: 2 (over y), ctx: 4 (over z), section: 2 (over x), head: 2 (over core).
Axes of the slice: x: 2, y: 2, z: 4, core: 2. Of those that a mesh axis runs over, the one named last changes fastest.
Arguments:
- tokens: bfloat16 [4, 512, 2048], P('groups', 'ctx', 'head'), parts along dimension 0, may hold values from -20 to 20
- norm_gain: bfloat16 [2, 2048], P('section'), may hold values from 0.5 to 1.5
- w_query: bfloat16 [2, 2048, 256], P('section', None, 'head'), may hold values from -0.125 to 0.125
- w_key: bfloat16 [2, 2048, 256], P('section', None, 'head'), may hold values from -0.125 to 0.125
- w_value: bfloat16 [2, 2048, 2048], P('section', None, 'head'), may hold values from -0.125 to 0.125
- conv_query: bfloat16 [2, 4, 256], P('section', None, 'head'), may hold values from -3 to 3
- conv_key: bfloat16 [2, 4, 256], P('section', None, 'head'), may hold values from -3 to 3
- conv_value: bfloat16 [2, 4, 2048], P('section', None, 'head'), may hold values from -3 to 3
- value_gain: bfloat16 [2, 2048], P('section', 'head'), may hold values from 0.5 to 1.5
- w_out: bfloat16 [2, 2048, 2048], P('section', 'head'), may hold values from -0.125 to 0.125
- doc_start: int32 [4], P('groups'), parts along dimension 0, may hold values from 1 to 511
- pad_length: int32 [4], P('groups'), parts along dimension 0, may hold values from 0 to 255
Outputs:
- layer_outputs: bfloat16 [2, 4, 512, 2048], P('section', 'groups', 'ctx', 'head'), parts along dimension 1
There are 2 independent parts, one for each index of `groups`. A program takes and returns all parts, laid end to end along the dimension named above; an argument that names none is the same for every part. Nothing has to cross between parts.
All inputs are finite; a program needn't handle non-finite values.
Results may differ from a plain program's by a relative error of at most 0.0061.
Values may be sent and summed in bfloat16 or wider, within the bound.
A program may use at most 128 MiB of HBM per device.

v0:
```python
import math

import jax
import jax.numpy as jnp
import numpy as np
from jax import lax
from jax.sharding import PartitionSpec as P

HD = 128


norm_eps = 1e-06


def passed_along(block, axis, distance):
    devices = range(lax.axis_size(axis))
    route = [(i - distance, i) for i in devices if i - distance in devices]
    return lax.ppermute(block, axis, route)


def entering(value, axis, join, neutral):
    count, mine = (lax.axis_size(axis), lax.axis_index(axis))
    pieces = jax.tree.map(lambda part: lax.all_gather(part, axis), value)
    so_far = jax.tree.map(
        lambda part, zero: jnp.full_like(part, 0) + jnp.asarray(zero, part.dtype), value, neutral
    )

    def lap(position, so_far):
        longer = join(so_far, jax.tree.map(lambda part: part[position], pieces))
        return jax.tree.map(lambda new, old: jnp.where(position < mine, new, old), longer, so_far)

    return lax.fori_loop(0, count - 1, lap, so_far)


def pair_tables(feat_width):
    left_list = []
    right_list = []
    weight_list = []
    for left_pos in range(feat_width):
        for right_pos in range(left_pos, feat_width):
            left_list.append(left_pos)
            right_list.append(right_pos)
            if left_pos == right_pos:
                weight_list.append(1.0 / math.sqrt(2.0 * feat_width))
            else:
                weight_list.append(1.0 / math.sqrt(feat_width))
    return (np.array(left_list, np.int32), np.array(right_list, np.int32), weight_list)


def taylor_columns(vectors):
    feat_width = vectors.shape[1]
    left_index, right_index, weight_list = pair_tables(feat_width)
    pair_weight = jnp.asarray(weight_list, dtype=jnp.float32)
    constant = jnp.ones((vectors.shape[0], 1, vectors.shape[2]), jnp.float32)
    linear = vectors * (1.0 / feat_width**0.25)
    quadratic = vectors[:, left_index, :] * vectors[:, right_index, :] * pair_weight[None, :, None]
    return jnp.concatenate([constant, linear, quadratic], axis=1)


def normed_rows(hidden, gain):
    row_values = hidden.astype(jnp.float32)
    mean_square = jnp.mean(row_values * row_values, axis=-1, keepdims=True)
    return (row_values * lax.rsqrt(mean_square + norm_eps) * gain.astype(jnp.float32)).astype(
        jnp.bfloat16
    )


def short_conv(extended, tap_weights, positions, boundary):
    tap_count = tap_weights.shape[0]
    row_count = extended.shape[0] - tap_count + 1
    summed = jnp.zeros((row_count, extended.shape[1]), jnp.float32)
    after_start = positions >= boundary
    for offset in range(tap_count):
        source = extended[tap_count - 1 - offset : tap_count - 1 - offset + row_count].astype(
            jnp.float32
        )
        earlier_side = positions - offset >= boundary
        keep_rows = (earlier_side == after_start).astype(jnp.float32)
        summed = summed + tap_weights[offset].astype(jnp.float32) * source * keep_rows[:, None]
    return summed


def head_columns(rows_in, head_count):
    return jnp.transpose(rows_in.reshape(rows_in.shape[0], head_count, -1), (1, 2, 0))


def mix_rows(queries, key_vals, values, positions, boundary, carried, value_gain):
    row_count = queries.shape[0]
    head_count = values.shape[1] // HD
    query_cols = head_columns(queries, head_count)
    key_cols = head_columns(key_vals, head_count)
    value_heads = values.reshape(row_count, head_count, HD)
    feat_width = query_cols.shape[1]
    scores = jnp.einsum(
        "hdi,hdj->hij", query_cols, key_cols, precision=lax.Precision.HIGHEST
    ) / math.sqrt(feat_width)
    after_start = positions >= boundary
    allowed = (positions[None, :] <= positions[:, None]) & (
        after_start[None, :] == after_start[:, None]
    )
    weights = jnp.where(allowed[None], 1.0 + scores + 0.5 * scores * scores, 0.0).astype(
        jnp.bfloat16
    )
    local_part = jnp.einsum(
        "hij,jhd->ihd", weights, value_heads, preferred_element_type=jnp.float32
    )
    block_start = positions[0]
    use_carried = (positions < boundary) | (boundary < block_start)
    query_feats = taylor_columns(query_cols)
    far_part = jnp.einsum("hfi,hfd->ihd", query_feats, carried, precision=lax.Precision.HIGHEST)
    far_part = far_part * use_carried.astype(jnp.float32)[:, None, None]
    numerator = local_part + far_part
    mean_square = jnp.mean(numerator * numerator, axis=-1, keepdims=True)
    scaled = numerator * lax.rsqrt(mean_square + norm_eps)
    return (scaled.reshape(row_count, -1) * value_gain.astype(jnp.float32)).astype(jnp.bfloat16)


def local_state(key_vals, values, positions, boundary):
    row_count = key_vals.shape[0]
    head_count = values.shape[1] // HD
    key_cols = head_columns(key_vals, head_count)
    value_heads = values.reshape(row_count, head_count, HD)
    block_start = positions[0]
    reset_here = (boundary >= block_start) & (boundary < block_start + row_count)
    keep_keys = (positions >= boundary) | jnp.logical_not(reset_here)
    key_feats = (taylor_columns(key_cols) * keep_keys.astype(jnp.float32)[None, None, :]).astype(
        jnp.bfloat16
    )
    block_state = jnp.einsum(
        "hfj,jhd->hfd", key_feats, value_heads, preferred_element_type=jnp.float32
    )
    return (block_state, reset_here)


def chain_combine(earlier, later):
    return (jnp.maximum(earlier[0], later[0]), later[1] + (1.0 - later[0]) * earlier[1])


def project_rows(rows_in, weight_matrix):
    return jnp.dot(rows_in, weight_matrix, preferred_element_type=jnp.float32).astype(jnp.bfloat16)


def local(
    tokens,
    norm_gain,
    w_query,
    w_key,
    w_value,
    conv_query,
    conv_key,
    conv_value,
    value_gain,
    w_out,
    doc_start,
    pad_length,
):
    micro_count = tokens.shape[0]
    span_rows = tokens.shape[1]
    half_width = tokens.shape[2]
    section_count = lax.axis_size("section")
    section_pos = lax.axis_index("section")
    block_start = lax.axis_index("ctx") * span_rows
    positions = block_start + jnp.arange(span_rows, dtype=jnp.int32)
    window_rows = span_rows * lax.axis_size("ctx")
    rim_rows = conv_query.shape[1] - 1
    tick_count = micro_count + section_count - 1
    received = jnp.zeros_like(tokens[0])
    outputs = jnp.zeros((1, micro_count, span_rows, half_width), jnp.bfloat16)
    slot_ids = jnp.arange(micro_count, dtype=jnp.int32)
    for tick_pos in range(tick_count):
        micro_slot = tick_pos - section_pos
        safe_slot = jnp.clip(micro_slot, 0, micro_count - 1)
        boundary = doc_start[safe_slot]
        pad_count = pad_length[safe_slot]
        first_input = tokens[min(tick_pos, micro_count - 1)]
        layer_input = jnp.where(section_pos == 0, first_input, received)
        full_rows = lax.all_gather(layer_input, "head", axis=1, tiled=True)
        normed = normed_rows(full_rows, norm_gain[0])
        proj_query = project_rows(normed, w_query[0])
        proj_key = project_rows(normed, w_key[0])
        proj_value = project_rows(normed, w_value[0])
        rim_query, rim_key, rim_value = passed_along(
            (
                proj_query[span_rows - rim_rows :],
                proj_key[span_rows - rim_rows :],
                proj_value[span_rows - rim_rows :],
            ),
            "ctx",
            1,
        )
        queries = short_conv(
            jnp.concatenate([rim_query, proj_query], axis=0), conv_query[0], positions, boundary
        )
        key_vals = short_conv(
            jnp.concatenate([rim_key, proj_key], axis=0), conv_key[0], positions, boundary
        )
        values = short_conv(
            jnp.concatenate([rim_value, proj_value], axis=0), conv_value[0], positions, boundary
        ).astype(jnp.bfloat16)
        block_state, reset_here = local_state(key_vals, values, positions, boundary)
        reset_flag = jnp.reshape(reset_here.astype(jnp.float32), (1,))
        start_flag = jnp.zeros((1,), jnp.float32)
        empty_state = jnp.zeros_like(block_state)
        prior_flag, carried = entering(
            (reset_flag, block_state), "ctx", chain_combine, (start_flag, empty_state)
        )
        mixed_rows = mix_rows(
            queries, key_vals, values, positions, boundary, carried, value_gain[0]
        )
        projected = jnp.dot(mixed_rows, w_out[0], preferred_element_type=jnp.float32)
        valid_rows = (positions < window_rows - pad_count).astype(jnp.float32)[:, None]
        update = lax.psum_scatter(projected, "head", scatter_dimension=1, tiled=True)
        output_half = (layer_input.astype(jnp.float32) + update * valid_rows).astype(jnp.bfloat16)
        outputs = jnp.where(
            (slot_ids == micro_slot)[None, :, None, None], output_half[None, None], outputs
        )
        if tick_pos + 1 < tick_count:
            received = passed_along(output_half, "section", 1)
    return outputs


def solution(mesh):
    return jax.shard_map(
        local,
        mesh=mesh,
        in_specs=(
            P("groups", "ctx", "head"),
            P("section", None),
            P("section", None, "head"),
            P("section", None, "head"),
            P("section", None, "head"),
            P("section", None, "head"),
            P("section", None, "head"),
            P("section", None, "head"),
            P("section", "head"),
            P("section", "head", None),
            P("groups"),
            P("groups"),
        ),
        out_specs=P("section", "groups", "ctx", "head"),
        check_vma=False,
    )
```

profile of v0, /device:TPU:27, one launch (start us, length us, event | category | flops | bytes accessed | tf_op | source)
XLA Modules:
  0.0 346.9 jit_solution(5094619399832225111)
XLA Ops:
  7.7 2.6 all-gather
  11.6 1.3 collective-permute-start.2
  12.9 1.4 convolution_convert_fusion.5
  14.4 1.3 collective-permute-start.1
  17.8 1.3 collective-permute-start
  24.3 1.2 or_convert_fusion.5
  29.8 1.9 fusion.106
  32.7 1.2 copy.99
  39.0 11.9 %all-reduce.3 = (f32[4]{0:T(128)S(1)}, f32[4]{0:T(128)}, f32[4]{0:T(128)}) all-reduce(f32[4]{0:T(128)S(1)} %dynamic-update-slice, f32[4]{0:T(128)S(1)} %dynamic-update-slice.1, f32[4]{0:T(128)S(1)} %dynamic-update-slice.2), channel_id=1, replica_groups=mesh['groups'=2,'ctx'=4,'section'=2,'head'=2] {'ctx'}, use_global_device_ids=true, to_apply=%add | all-reduce | flops 12 | bytes 96
  56.3 33.1 %all-gather.8.cloned.1.call-done = f32[32,153,128]{2,0,1:T(8,128)} async-done(((f32[8,153,128]{2,0,1:T(8,128)}), f32[32,153,128]{2,0,1:T(8,128)}) %all-gather.8.cloned.1.call-update) | async-done | bytes 2506768 | tf_op jit(solution)/shard_map/all_gather | solution.py:23
  89.4 8.6 %while.42 = (s32[]{:T(128)}, f32[8,153,128]{2,1,0:T(8,128)S(1)}, s32[]{:T(128)}, f32[4,8,153,128]{3,1,0,2:T(8,128)}, f32[4,1]{0,1:T(1,128)S(1)}, /*index=5*/s32[]{:T(128)}, s32[]{:T(128)}) while((s32[]{:T(128)}, f32[8,153,128]{2,1,0:T(8,128)S(1)}, s32[]{:T(128)}, f32[4,8,153,128]{3,1,0,2:T(8,128)}, f32[4,1]{0,1:T(1,128)S(1)}, ...), condition=%wide.region_2.3_spmd.clone, body=%wide.region_1.2_spmd.clone.sunk | while | flops 626693 | bytes 3133557 | solution.py:32
  98.0 1.9 multiply_reduce_fusion.2
  100.2 3.9 %fusion.10 = f32[128,2048]{1,0:T(8,128)} fusion(bf16[128,1024]{0,1:T(8,128)(2,1)S(1)} %bitcast.208, bf16[1,1024,2048]{2,1,0:T(8,128)(2,1)} %param.57), kind=kOutput, calls=%fused_computation.31 | convolution fusion | flops 536870912 | bytes 5505024 | tf_op jit(solution)/shard_map/dot_general | solution.py:210
  105.9 8.4 %reduce-scatter.4.cloned.1.call-done = f32[128,1024]{1,0:T(8,128)} async-done(((f32[128,2048]{1,0:T(8,128)}), f32[128,1024]{1,0:T(8,128)}) %reduce-scatter.4.cloned.1.call-update) | async-done | bytes 524304 | tf_op jit(solution)/shard_map/reduce_scatter | solution.py:212
  115.5 1.3 collective-permute-start.3
  119.1 6.0 %collective-permute-done.3 = bf16[128,1024]{1,0:T(8,128)(2,1)S(1)} collective-permute-done((bf16[128,1024]{1,0:T(8,128)(2,1)S(1)}, bf16[128,1024]{1,0:T(8,128)(2,1)S(1)}, u32[]{:S(2)}, u32[]{:S(2)}) %collective-permute-start.3) | collective-permute-done | bytes 262176 | tf_op jit(solution)/shard_map/ppermute | solution.py:18
  125.2 3.0 all_gather.40
  128.8 3.0 fusion.27
  131.8 1.3 collective-permute-start.6
  133.5 1.3 collective-permute-start.5
  135.4 1.3 collective-permute-start.4
  139.8 1.6 gather_fusion.7
  141.4 1.4 fusion.62
  142.9 1.2 fusion.107
  145.1 1.2 copy.113
  148.9 52.6 %all-gather.10.cloned.1.call-done = f32[32,153,128]{2,0,1:T(8,128)} async-done(((f32[8,153,128]{2,0,1:T(8,128)}), f32[32,153,128]{2,0,1:T(8,128)}) %all-gather.10.cloned.1.call-update) | async-done | bytes 2506768 | tf_op jit(solution)/shard_map/all_gather | solution.py:23
  201.6 9.7 %while.43 = (s32[]{:T(128)}, f32[8,153,128]{2,1,0:T(8,128)S(1)}, s32[]{:T(128)}, f32[4,8,153,128]{3,1,0,2:T(8,128)}, f32[4,1]{0,1:T(1,128)}, /*index=5*/s32[]{:T(128)}, s32[]{:T(128)}) while((s32[]{:T(128)}, f32[8,153,128]{2,1,0:T(8,128)S(1)}, s32[]{:T(128)}, f32[4,8,153,128]{3,1,0,2:T(8,128)}, f32[4,1]{0,1:T(1,128)}, ...), condition=%wide.region_7.8_spmd.clone, body=%wide.region_6.7_spmd.clone.sunk | while | flops 626693 | bytes 3133557 | solution.py:32
  202.7 1.2 fusion.170
  205.9 1.2 fusion.170
  209.2 1.2 fusion.170
  211.3 1.9 multiply_reduce_fusion.1
  213.5 3.9 %fusion.8 = f32[128,2048]{1,0:T(8,128)} fusion(bf16[128,1024]{0,1:T(8,128)(2,1)S(1)} %bitcast.209, bf16[1,1024,2048]{2,1,0:T(8,128)(2,1)} %param.57), kind=kOutput, calls=%fused_computation.29 | convolution fusion | flops 536870912 | bytes 5505024 | tf_op jit(solution)/shard_map/dot_general | solution.py:210
  219.3 8.3 %reduce-scatter.6.cloned.1.call-done = f32[128,1024]{1,0:T(8,128)} async-done(((f32[128,2048]{1,0:T(8,128)}), f32[128,1024]{1,0:T(8,128)}) %reduce-scatter.6.cloned.1.call-update) | async-done | bytes 524304 | tf_op jit(solution)/shard_map/reduce_scatter | solution.py:212
  228.8 1.3 collective-permute-start.7
  232.4 5.9 %collective-permute-done.7 = bf16[128,1024]{1,0:T(8,128)(2,1)S(1)} collective-permute-done((bf16[128,1024]{1,0:T(8,128)(2,1)S(1)}, bf16[128,1024]{1,0:T(8,128)(2,1)S(1)}, u32[]{:S(2)}, u32[]{:S(2)}) %collective-permute-start.7) | collective-permute-done | bytes 262176 | tf_op jit(solution)/shard_map/ppermute | solution.py:18
  238.4 2.8 all_gather.44
  241.9 3.0 fusion.30
  244.9 1.3 collective-permute-start.10
  246.6 1.3 collective-permute-start.9
  248.5 1.5 collective-permute-start.8
  253.1 1.6 gather_fusion.11
  254.7 1.4 fusion.58
  257.5 1.2 copy.127
  261.4 52.0 %all-gather.12.cloned.1.call-done = f32[32,153,128]{2,0,1:T(8,128)} async-done(((f32[8,153,128]{2,0,1:T(8,128)}), f32[32,153,128]{2,0,1:T(8,128)}) %all-gather.12.cloned.1.call-update) | async-done | bytes 2506768 | tf_op jit(solution)/shard_map/all_gather | solution.py:23
  313.4 8.2 %while.44 = (s32[]{:T(128)}, f32[8,153,128]{2,1,0:T(8,128)S(1)}, s32[]{:T(128)}, f32[4,8,153,128]{3,1,0,2:T(8,128)}, f32[4,1]{0,1:T(1,128)S(1)}, /*index=5*/s32[]{:T(128)}, s32[]{:T(128)}) while((s32[]{:T(128)}, f32[8,153,128]{2,1,0:T(8,128)S(1)}, s32[]{:T(128)}, f32[4,8,153,128]{3,1,0,2:T(8,128)}, f32[4,1]{0,1:T(1,128)S(1)}, ...), condition=%wide.region_12.13_spmd.clone, body=%wide.region_11.12_spmd.clone.sunk | while | flops 626693 | bytes 3133557 | solution.py:32
  321.6 1.9 multiply_reduce_fusion
  323.8 3.9 %fusion.6 = f32[128,2048]{1,0:T(8,128)} fusion(bf16[128,1024]{0,1:T(8,128)(2,1)S(1)} %bitcast.207, bf16[1,1024,2048]{2,1,0:T(8,128)(2,1)} %param.57), kind=kOutput, calls=%fused_computation.27 | convolution fusion | flops 536870912 | bytes 5505024 | tf_op jit(solution)/shard_map/dot_general | solution.py:210
  328.4 9.5 %reduce-scatter.8.cloned.1.call-done = f32[128,1024]{1,0:T(8,128)} async-done(((f32[128,2048]{1,0:T(8,128)}), f32[128,1024]{1,0:T(8,128)}) %reduce-scatter.8.cloned.1.call-update) | async-done | bytes 524304 | tf_op jit(solution)/shard_map/reduce_scatter | solution.py:212
  (346 shorter events, 70.6 us)
Async XLA Ops:
  6.5 82.9 %all-gather.8.cloned.1.call-start = ((), (), s32[]{:S(2)}) async-start(), calls=%async_computation.6 | async-start | bytes 3133440 | tf_op jit(solution)/shard_map/all_gather | solution.py:23
  10.3 13.0 %copy-start.76 = (bf16[1,4,128]{2,1,0:T(4,128)(2,1)S(1)}, bf16[1,4,128]{2,1,0:T(4,128)(2,1)}, u32[]{:S(2)}) copy-start(bf16[1,4,128]{2,1,0:T(4,128)(2,1)} %param.54) | copy-start | bytes 3076
  10.3 13.0 %copy-start.83 = (s32[136]{0:T(256)S(1)}, s32[136]{0:T(256)}, u32[]{:S(2)}) copy-start(s32[136]{0:T(256)} %constant.180) | copy-start | bytes 1636
  10.3 13.1 %copy-start.82 = (s32[136]{0:T(256)S(1)}, s32[136]{0:T(256)}, u32[]{:S(2)}) copy-start(s32[136]{0:T(256)} %constant.181) | copy-start | bytes 1636
  10.3 13.1 %copy-start.77 = (bf16[1,4,128]{2,1,0:T(4,128)(2,1)S(1)}, bf16[1,4,128]{2,1,0:T(4,128)(2,1)}, u32[]{:S(2)}) copy-start(bf16[1,4,128]{2,1,0:T(4,128)(2,1)} %param.53) | copy-start | bytes 3076
  10.3 13.2 %copy-start.19 = (bf16[1,4,1024]{2,1,0:T(4,128)(2,1)S(1)}, bf16[1,4,1024]{2,1,0:T(4,128)(2,1)}, u32[]{:S(2)}) copy-start(bf16[1,4,1024]{2,1,0:T(4,128)(2,1)} %param.55) | copy-start | bytes 24580
  11.6 13.9 %collective-permute-start.2 = (bf16[3,128]{1,0:T(4,128)(2,1)S(1)}, bf16[3,128]{1,0:T(4,128)(2,1)S(1)}, u32[]{:S(2)}, u32[]{:S(2)}) collective-permute-start(bf16[3,128]{1,0:T(4,128)(2,1)S(1)} %slice.280), channel_id=1, source_target_pairs={{0,4},{4,8},{8,12},{1,5},{5,9},{9,13},{2,6},{6,10},{10,14},{3,7},{... | collective-permute-start | bytes 2312 | tf_op jit(solution)/shard_map/ppermute | solution.py:18
  14.3 15.0 %copy-start.26 = (f32[136]{0:T(256)S(1)}, f32[136]{0:T(256)}, u32[]{:S(2)}) copy-start(f32[136]{0:T(256)} %constant.165.clone) | copy-start | bytes 1636
  14.4 13.0 %collective-permute-start.1 = (bf16[3,128]{1,0:T(4,128)(2,1)S(1)}, bf16[3,128]{1,0:T(4,128)(2,1)S(1)}, u32[]{:S(2)}, u32[]{:S(2)}) collective-permute-start(bf16[3,128]{1,0:T(4,128)(2,1)S(1)} %slice.275), channel_id=1, source_target_pairs={{0,4},{4,8},{8,12},{1,5},{5,9},{9,13},{2,6},{6,10},{10,14},{3,7},{... | collective-permute-start | bytes 2312 | tf_op jit(solution)/shard_map/ppermute | solution.py:18
  17.8 12.0 %collective-permute-start = (bf16[3,1024]{1,0:T(4,128)(2,1)}, bf16[3,1024]{1,0:T(4,128)(2,1)}, u32[]{:S(2)}, u32[]{:S(2)}) collective-permute-start(bf16[3,1024]{1,0:T(4,128)(2,1)} %slice.270), channel_id=1, source_target_pairs={{0,4},{4,8},{8,12},{1,5},{5,9},{9,13},{2,6},{6,10},{10,14},{3,7},{... | collective-permute-start | bytes 18440 | tf_op jit(solution)/shard_map/ppermute | solution.py:18
  28.6 23.0 %copy-start.75 = (bf16[1,1024]{1,0:T(2,128)(2,1)S(1)}, bf16[1,1024]{1,0:T(2,128)(2,1)}, u32[]{:S(2)}) copy-start(bf16[1,1024]{1,0:T(2,128)(2,1)} %param.56) | copy-start | bytes 6148
  34.0 80.4 %reduce-scatter.4.cloned.1.call-start = ((), (), s32[]{:S(2)}) async-start(), calls=%async_computation.3 | async-start | bytes 1572864 | tf_op jit(solution)/shard_map/reduce_scatter | solution.py:212
  100.0 14.4 %copy-start.2 = (bf16[2,128,1024]{2,1,0:T(8,128)(2,1)S(1)}, bf16[2,128,1024]{2,1,0:T(8,128)(2,1)}, u32[]{:S(2)}) copy-start(bf16[2,128,1024]{2,1,0:T(8,128)(2,1)} %param.48) | copy-start | bytes 1572868
  104.1 97.5 %all-gather.10.cloned.1.call-start = ((), (), s32[]{:S(2)}) async-start(), calls=%async_computation.7 | async-start | bytes 3133440 | tf_op jit(solution)/shard_map/all_gather | solution.py:23
  105.3 33.4 %copy-start.63 = (f32[128]{0:T(128)}, f32[128]{0:T(128)S(1)}, u32[]{:S(2)}) copy-start(f32[128]{0:T(128)S(1)} %compare_convert_fusion.6) | copy-start | bytes 1540
  105.9 32.8 %copy-start.65 = (f32[128]{0:T(128)}, f32[128]{0:T(128)S(1)}, u32[]{:S(2)}) copy-start(f32[128]{0:T(128)S(1)} %compare_convert_fusion.7) | copy-start | bytes 1540
  115.5 16.3 %copy-start.5 = (bf16[128,1024]{1,0:T(8,128)(2,1)}, bf16[128,1024]{1,0:T(8,128)(2,1)S(1)}, u32[]{:S(2)}) copy-start(bf16[128,1024]{1,0:T(8,128)(2,1)S(1)} %fusion.69) | copy-start | bytes 786436
  115.5 9.6 %collective-permute-start.3 = (bf16[128,1024]{1,0:T(8,128)(2,1)S(1)}, bf16[128,1024]{1,0:T(8,128)(2,1)S(1)}, u32[]{:S(2)}, u32[]{:S(2)}) collective-permute-start(bf16[128,1024]{1,0:T(8,128)(2,1)S(1)} %fusion.69), channel_id=1, source_target_pairs={{0,2},{1,3},{4,6},{5,7},{8,10},{9,11},{12,14},{13,15},{16,18},{17,... | collective-permute-start | bytes 786440 | tf_op jit(solution)/shard_map/ppermute | solution.py:18
  117.4 21.3 %copy-start.71 = (f32[128]{0:T(128)}, f32[128]{0:T(128)S(1)}, u32[]{:S(2)}) copy-start(f32[128]{0:T(128)S(1)} %compare_convert_fusion.8) | copy-start | bytes 1540
  118.0 20.7 %copy-start.73 = (f32[128]{0:T(128)}, f32[128]{0:T(128)S(1)}, u32[]{:S(2)}) copy-start(f32[128]{0:T(128)S(1)} %compare_convert_fusion.9) | copy-start | bytes 1540
  119.1 14.0 %copy-start.84 = (bf16[1,2048,128]{2,1,0:T(8,128)(2,1)S(1)}, bf16[1,2048,128]{2,1,0:T(8,128)(2,1)}, u32[]{:S(2)}) copy-start(bf16[1,2048,128]{2,1,0:T(8,128)(2,1)} %param.50) | copy-start | bytes 1572868
  128.7 9.9 %copy-start.30 = (f32[128]{0:T(128)S(1)}, f32[128]{0:T(128)}, u32[]{:S(2)}) copy-start(f32[128]{0:T(128)} %copy-done.29) | copy-start | bytes 1540
  128.8 9.9 %copy-start.33 = (f32[128]{0:T(128)S(1)}, f32[128]{0:T(128)}, u32[]{:S(2)}) copy-start(f32[128]{0:T(128)} %copy-done.32) | copy-start | bytes 1540
  128.8 9.9 %copy-start.36 = (f32[128]{0:T(128)S(1)}, f32[128]{0:T(128)}, u32[]{:S(2)}) copy-start(f32[128]{0:T(128)} %copy-done.35) | copy-start | bytes 1540
  131.8 4.9 %collective-permute-start.6 = (bf16[3,128]{1,0:T(4,128)(2,1)S(1)}, bf16[3,128]{1,0:T(4,128)(2,1)S(1)}, u32[]{:S(2)}, u32[]{:S(2)}) collective-permute-start(bf16[3,128]{1,0:T(4,128)(2,1)S(1)} %slice.295), channel_id=1, source_target_pairs={{0,4},{4,8},{8,12},{1,5},{5,9},{9,13},{2,6},{6,10},{10,14},{3,7},{... | collective-permute-start | bytes 2312 | tf_op jit(solution)/shard_map/ppermute | solution.py:18
  133.5 5.1 %collective-permute-start.5 = (bf16[3,128]{1,0:T(4,128)(2,1)S(1)}, bf16[3,128]{1,0:T(4,128)(2,1)S(1)}, u32[]{:S(2)}, u32[]{:S(2)}) collective-permute-start(bf16[3,128]{1,0:T(4,128)(2,1)S(1)} %slice.290), channel_id=1, source_target_pairs={{0,4},{4,8},{8,12},{1,5},{5,9},{9,13},{2,6},{6,10},{10,14},{3,7},{... | collective-permute-start | bytes 2312 | tf_op jit(solution)/shard_map/ppermute | solution.py:18
  135.4 7.5 %collective-permute-start.4 = (bf16[3,1024]{1,0:T(4,128)(2,1)}, bf16[3,1024]{1,0:T(4,128)(2,1)}, u32[]{:S(2)}, u32[]{:S(2)}) collective-permute-start(bf16[3,1024]{1,0:T(4,128)(2,1)} %slice.285), channel_id=1, source_target_pairs={{0,4},{4,8},{8,12},{1,5},{5,9},{9,13},{2,6},{6,10},{10,14},{3,7},{... | collective-permute-start | bytes 18440 | tf_op jit(solution)/shard_map/ppermute | solution.py:18
  146.4 81.2 %reduce-scatter.6.cloned.1.call-start = ((), (), s32[]{:S(2)}) async-start(), calls=%async_computation.4 | async-start | bytes 1572864 | tf_op jit(solution)/shard_map/reduce_scatter | solution.py:212
  213.2 25.2 %copy-start.3 = (bf16[2,128,1024]{2,1,0:T(8,128)(2,1)S(1)}, bf16[2,128,1024]{2,1,0:T(8,128)(2,1)}, u32[]{:S(2)}) copy-start(bf16[2,128,1024]{2,1,0:T(8,128)(2,1)} %param.48) | copy-start | bytes 1572868
  217.4 96.0 %all-gather.12.cloned.1.call-start = ((), (), s32[]{:S(2)}) async-start(), calls=%async_computation.8 | async-start | bytes 3133440 | tf_op jit(solution)/shard_map/all_gather | solution.py:23
  218.7 33.2 %copy-start.55 = (f32[128]{0:T(128)}, f32[128]{0:T(128)S(1)}, u32[]{:S(2)}) copy-start(f32[128]{0:T(128)S(1)} %compare_convert_fusion.1) | copy-start | bytes 1540
  219.3 32.6 %copy-start.57 = (f32[128]{0:T(128)}, f32[128]{0:T(128)S(1)}, u32[]{:S(2)}) copy-start(f32[128]{0:T(128)S(1)} %compare_convert_fusion.2) | copy-start | bytes 1540
  228.8 16.1 %copy-start.7 = (bf16[128,1024]{1,0:T(8,128)(2,1)}, bf16[128,1024]{1,0:T(8,128)(2,1)S(1)}, u32[]{:S(2)}) copy-start(bf16[128,1024]{1,0:T(8,128)(2,1)S(1)} %add_convert_fusion.2) | copy-start | bytes 786436
  228.8 9.6 %collective-permute-start.7 = (bf16[128,1024]{1,0:T(8,128)(2,1)S(1)}, bf16[128,1024]{1,0:T(8,128)(2,1)S(1)}, u32[]{:S(2)}, u32[]{:S(2)}) collective-permute-start(bf16[128,1024]{1,0:T(8,128)(2,1)S(1)} %add_convert_fusion.2), channel_id=1, source_target_pairs={{0,2},{1,3},{4,6},{5,7},{8,10},{9,11},{12,14},{13,15},{16,18},{17,... | collective-permute-start | bytes 786440 | tf_op jit(solution)/shard_map/ppermute | solution.py:18
  230.7 21.2 %copy-start.59 = (f32[128]{0:T(128)}, f32[128]{0:T(128)S(1)}, u32[]{:S(2)}) copy-start(f32[128]{0:T(128)S(1)} %compare_convert_fusion.3) | copy-start | bytes 1540
  231.3 20.6 %copy-start.61 = (f32[128]{0:T(128)}, f32[128]{0:T(128)S(1)}, u32[]{:S(2)}) copy-start(f32[128]{0:T(128)S(1)} %compare_convert_fusion.4) | copy-start | bytes 1540
  232.4 13.7 %copy-start.85 = (bf16[1,2048,128]{2,1,0:T(8,128)(2,1)S(1)}, bf16[1,2048,128]{2,1,0:T(8,128)(2,1)}, u32[]{:S(2)}) copy-start(bf16[1,2048,128]{2,1,0:T(8,128)(2,1)} %param.50) | copy-start | bytes 1572868
  241.8 10.1 %copy-start.31 = (f32[128]{0:T(128)S(1)}, f32[128]{0:T(128)}, u32[]{:S(2)}) copy-start(f32[128]{0:T(128)} %copy-done.29) | copy-start | bytes 1540
  241.8 10.1 %copy-start.34 = (f32[128]{0:T(128)S(1)}, f32[128]{0:T(128)}, u32[]{:S(2)}) copy-start(f32[128]{0:T(128)} %copy-done.32) | copy-start | bytes 1540
  241.9 10.1 %copy-start.37 = (f32[128]{0:T(128)S(1)}, f32[128]{0:T(128)}, u32[]{:S(2)}) copy-start(f32[128]{0:T(128)} %copy-done.35) | copy-start | bytes 1540
  241.9 10.1 %copy-start.40 = (f32[128]{0:T(128)S(1)}, f32[128]{0:T(128)}, u32[]{:S(2)}) copy-start(f32[128]{0:T(128)} %copy-done.38) | copy-start | bytes 1540
  244.9 5.1 %collective-permute-start.10 = (bf16[3,128]{1,0:T(4,128)(2,1)S(1)}, bf16[3,128]{1,0:T(4,128)(2,1)S(1)}, u32[]{:S(2)}, u32[]{:S(2)}) collective-permute-start(bf16[3,128]{1,0:T(4,128)(2,1)S(1)} %slice.310), channel_id=1, source_target_pairs={{0,4},{4,8},{8,12},{1,5},{5,9},{9,13},{2,6},{6,10},{10,14},{3,7},{... | collective-permute-start | bytes 2312 | tf_op jit(solution)/shard_map/ppermute | solution.py:18
  246.6 5.3 %collective-permute-start.9 = (bf16[3,128]{1,0:T(4,128)(2,1)S(1)}, bf16[3,128]{1,0:T(4,128)(2,1)S(1)}, u32[]{:S(2)}, u32[]{:S(2)}) collective-permute-start(bf16[3,128]{1,0:T(4,128)(2,1)S(1)} %slice.305), channel_id=1, source_target_pairs={{0,4},{4,8},{8,12},{1,5},{5,9},{9,13},{2,6},{6,10},{10,14},{3,7},{... | collective-permute-start | bytes 2312 | tf_op jit(solution)/shard_map/ppermute | solution.py:18
  248.5 7.6 %collective-permute-start.8 = (bf16[3,1024]{1,0:T(4,128)(2,1)}, bf16[3,1024]{1,0:T(4,128)(2,1)S(1)}, u32[]{:S(2)}, u32[]{:S(2)}) collective-permute-start(bf16[3,1024]{1,0:T(4,128)(2,1)} %slice.300), channel_id=1, source_target_pairs={{0,4},{4,8},{8,12},{1,5},{5,9},{9,13},{2,6},{6,10},{10,14},{3,7},{... | collective-permute-start | bytes 18440 | tf_op jit(solution)/shard_map/ppermute | solution.py:18
  254.7 58.7 %copy-start.86 = (f32[4]{0:T(128)S(1)}, f32[4]{0:T(128)}, u32[]{:S(2)}) copy-start(f32[4]{0:T(128)} %get-tuple-element.391) | copy-start | bytes 52
  258.7 79.2 %reduce-scatter.8.cloned.1.call-start = ((), (), s32[]{:S(2)}) async-start(), calls=%async_computation.5 | async-start | bytes 1572864 | tf_op jit(solution)/shard_map/reduce_scatter | solution.py:212
  323.6 15.6 %copy-start.6 = (bf16[128,1024]{1,0:T(8,128)(2,1)S(1)}, bf16[128,1024]{1,0:T(8,128)(2,1)}, u32[]{:S(2)}) copy-start(bf16[128,1024]{1,0:T(8,128)(2,1)} %copy-done.5) | copy-start | bytes 786436
  323.6 15.6 %copy-start.8 = (bf16[128,1024]{1,0:T(8,128)(2,1)S(1)}, bf16[128,1024]{1,0:T(8,128)(2,1)}, u32[]{:S(2)}) copy-start(bf16[128,1024]{1,0:T(8,128)(2,1)} %copy-done.7) | copy-start | bytes 786436
  (57 other events, 355.9 us)
Sparse Core Ops, SparseCore 0:
  34.1 55.3 all-gather.7
  104.2 10.0 reduce-scatter.3
  146.5 55.0 all-gather.9
  217.5 10.0 reduce-scatter.5
  258.8 54.4 all-gather.11
  327.8 10.0 reduce-scatter.7
where the time goes:
time: 350 us; the launch traced here: 347 us
  waiting for transfers between devices  176 us (50%)
  other arithmetic  46.8 us (13%)
  matrix products  34.3 us (10%)
  local copies, waits for them, and re-layouts  31.5 us (9%)
  between operations  23 us (7%)
  blocking collectives  20.3 us (6%)
  starting transfers between devices  14.6 us (4%)
    all_gather x3, waiting for transfers between devices, entering(): pieces = jax.tree.map(lambda part: lax.all_gather(part, axis), value)  138 us
    reduce_scatter x3, waiting for transfers between devices, local(): lax.psum_scatter(projected, 'head', scatter_dimension=1, tiled=True)  26.3 us
    ppermute x11, starting transfers between devices, passed_along(): return lax.ppermute(block, axis, route)  14.4 us
    ppermute x11, waiting for transfers between devices, passed_along(): return lax.ppermute(block, axis, route)  12 us
    unnamed x1, blocking collectives  11.9 us
    dot_general x3, matrix products, local(): jnp.dot(mixed_rows, w_out[0], preferred_element_type=jnp.float32)  11.7 us
    dynamic_slice x9, local copies, waits for them, and re-layouts, lap(): longer = join(so_far, jax.tree.map(lambda part: part[position], pieces))  10.1 us
    dot_general x9, matrix products, project_rows(): jnp.dot(rows_in, weight_matrix, preferred_element_type=jnp.float32)  9.96 us
  transfers between devices with their start and end apart: 17, of which 8 were waited for; matrix products, arithmetic and copies ran while one was open for 12% of the time, Pallas kernels for 0%

commit v1 on v0

v1 whole, which is shorter than its diff:
```python
import math

import jax
import jax.numpy as jnp
from jax import lax
from jax.experimental import pallas as pl
from jax.experimental.pallas import tpu as pltpu
from jax.sharding import PartitionSpec as P

HD = 128
FD = 16
FROWS = 160
CHUNK = 256
EPS = 1e-06
MESH = pl.DeviceIdType.MESH
F32 = jnp.float32
BF16 = jnp.bfloat16


def features(doubled, first):
    x = doubled[first + (pl.ds(0, FD), slice(None))]
    rows = [x * (1.0 / FD**0.25), x * x * (1.0 / math.sqrt(2.0 * FD))]
    for d in range(1, FD // 2):
        rows.append(x * doubled[first + (pl.ds(d, FD), slice(None))] * (1.0 / math.sqrt(FD)))
    half = FD // 2
    rows.append(x[:half] * x[half:] * (1.0 / math.sqrt(FD)))
    lead = lax.broadcasted_iota(jnp.int32, (half, x.shape[1]), 0) == 0
    rows.append(jnp.where(lead, 1.0, 0.0))
    return jnp.concatenate(rows, axis=0)


def make_kernel(sizes):
    ctx_n, sec_n, windows, span, width, taps = sizes
    half = width // 2
    rows_n = windows * span
    heads = half // HD
    vchunks = half // CHUNK
    hop_lag = 2
    steps = heads + hop_lag * max(ctx_n - 2, 0)

    def kernel(
        start_ref, pad_ref, tok_ref, gain_ref, wq_ref, wk_ref, wv_ref, cq_ref, ck_ref, cv_ref, vg_ref, wo_ref,
        out_ref,
        w_all, wo_v, x_ref, n_ref, pr_ref, q3_ref, k3_ref, qt_ref, kt_ref, v_ref, bs_ref, got_ref, fwd_ref,
        num_ref, mix_ref, part_ref, other_ref,
        w_sem, x_send, x_recv, sec_send, sec_recv, halo_send, halo_recv, st_send, st_recv, p_send, p_recv,
    ):
        ctx = lax.axis_index("ctx")
        sec = lax.axis_index("section")
        core = lax.axis_index("head")
        mate = 1 - core

        loads = [
            pltpu.make_async_copy(wq_ref.at[0], w_all.at[:, pl.ds(0, HD)], w_sem.at[0]),
            pltpu.make_async_copy(wk_ref.at[0], w_all.at[:, pl.ds(HD, HD)], w_sem.at[1]),
        ]
        for j in range(vchunks):
            loads.append(
                pltpu.make_async_copy(
                    wv_ref.at[0, :, pl.ds(j * CHUNK, CHUNK)],
                    w_all.at[:, pl.ds((j + 1) * CHUNK, CHUNK)],
                    w_sem.at[2 + j],
                )
            )
        wo_load = pltpu.make_async_copy(wo_ref.at[0], wo_v, w_sem.at[2 + vchunks])
        for load in loads:
            load.start()
        wo_load.start()

        barrier = pltpu.get_barrier_semaphore()
        pl.semaphore_signal(barrier, inc=1, device_id={"head": mate}, device_id_type=MESH)

        @pl.when(ctx > 0)
        def _():
            pl.semaphore_signal(barrier, inc=1, device_id={"ctx": ctx - 1}, device_id_type=MESH)

        @pl.when(ctx < ctx_n - 1)
        def _():
            pl.semaphore_signal(barrier, inc=1, device_id={"ctx": ctx + 1}, device_id_type=MESH)

        @pl.when(sec > 0)
        def _():
            pl.semaphore_signal(barrier, inc=1, device_id={"section": sec - 1}, device_id_type=MESH)

        @pl.when(sec < sec_n - 1)
        def _():
            pl.semaphore_signal(barrier, inc=1, device_id={"section": sec + 1}, device_id_type=MESH)

        peers = (
            1
            + jnp.where(ctx > 0, 1, 0)
            + jnp.where(ctx < ctx_n - 1, 1, 0)
            + jnp.where(sec > 0, 1, 0)
            + jnp.where(sec < sec_n - 1, 1, 0)
        )
        pl.semaphore_wait(barrier, peers)

        def cols(j):
            return pl.ds(j * CHUNK, CHUNK)

        def section_copy(j):
            return pltpu.make_async_remote_copy(
                src_ref=out_ref.at[:, cols(j)],
                dst_ref=x_ref.at[core, :, cols(j)],
                send_sem=sec_send.at[j],
                recv_sem=sec_recv.at[j],
                device_id={"section": sec + 1},
                device_id_type=MESH,
            )

        def mate_copy(j):
            return pltpu.make_async_remote_copy(
                src_ref=x_ref.at[core, :, cols(j)],
                dst_ref=x_ref.at[core, :, cols(j)],
                send_sem=x_send.at[j],
                recv_sem=x_recv.at[j],
                device_id={"head": mate},
                device_id_type=MESH,
            )

        @pl.when(sec == 0)
        def _():
            x_ref[core] = tok_ref[...]

        for j in range(vchunks):

            @pl.when(sec > 0)
            def _():
                section_copy(j).wait_recv()

            mate_copy(j).start()

        first = ctx * span
        col_pos = first + lax.broadcasted_iota(jnp.int32, (span, HD), 0)
        lane_pos = first + lax.broadcasted_iota(jnp.int32, (1, span), 1)
        starts = [start_ref[m] for m in range(windows)]

        for j in range(vchunks):
            mate_copy(j).wait_recv()

        block = 32

        def norm_rows(i, carry):
            at = pl.ds(pl.multiple_of(i * block, block), block)
            left = x_ref[0, at, :].astype(F32)
            right = x_ref[1, at, :].astype(F32)
            square = jnp.sum(left * left, axis=1, keepdims=True) + jnp.sum(right * right, axis=1, keepdims=True)
            scale = lax.rsqrt(square * (1.0 / width) + EPS)
            n_ref[at, pl.ds(0, half)] = (left * scale * gain_ref[:, pl.ds(0, half)].astype(F32)).astype(BF16)
            n_ref[at, pl.ds(half, half)] = (right * scale * gain_ref[:, pl.ds(half, half)].astype(F32)).astype(BF16)
            return carry

        lax.fori_loop(0, rows_n // block, norm_rows, 0)

        def halo_copy(j):
            return pltpu.make_async_remote_copy(
                src_ref=pr_ref.at[:, pl.ds(span, 8), cols(j)],
                dst_ref=pr_ref.at[:, pl.ds(0, 8), cols(j)],
                send_sem=halo_send.at[j],
                recv_sem=halo_recv.at[j],
                device_id={"ctx": ctx + 1},
                device_id_type=MESH,
            )

        @pl.when(ctx == 0)
        def _():
            pr_ref[:, pl.ds(0, 8), :] = jnp.zeros((windows, 8, half + CHUNK), F32)

        for j in range(vchunks + 1):
            if j == 0:
                loads[0].wait()
                loads[1].wait()
            else:
                loads[1 + j].wait()
            got = jnp.dot(n_ref[...], w_all[:, cols(j)], preferred_element_type=F32).astype(BF16).astype(F32)
            for m in range(windows):
                pr_ref[m, pl.ds(8, span), cols(j)] = got[m * span : (m + 1) * span]

            @pl.when(ctx < ctx_n - 1)
            def _():
                halo_copy(j).start()

        def conv(m, at, taps_ref, tap_at):
            after = col_pos >= starts[m]
            total = None
            for j in range(taps):
                source = pr_ref[m, pl.ds(8 - j, span), at]
                term = taps_ref[0, pl.ds(j, 1), tap_at].astype(F32) * source
                if j:
                    same = (col_pos - j >= starts[m]) == after
                    term = jnp.where(same, term, 0.0)
                total = term if total is None else total + term
            return total

        def halo_wait(j):
            @pl.when(ctx > 0)
            def _():
                halo_copy(j).wait_recv()

        halo_wait(0)
        for m in range(windows):
            for which, taps_ref, wide_ref, turned_ref in ((0, cq_ref, q3_ref, qt_ref), (1, ck_ref, k3_ref, kt_ref)):
                part = conv(m, pl.ds(which * HD, HD), taps_ref, pl.ds(0, HD))
                high = part.astype(BF16)
                low = (part - high.astype(F32)).astype(BF16)
                wide_ref[m, :, pl.ds(0, HD)] = high
                wide_ref[m, :, pl.ds(HD, HD)] = high if which == 0 else low
                wide_ref[m, :, pl.ds(2 * HD, HD)] = low if which == 0 else high
                turned = jnp.transpose(part)
                for h in range(heads):
                    own = turned[h * FD : (h + 1) * FD]
                    turned_ref[m, h, pl.ds(0, FD), :] = own
                    turned_ref[m, h, pl.ds(FD, FD), :] = own

        for j in range(vchunks):
            halo_wait(1 + j)
            for m in range(windows):
                for c in range(CHUNK // HD):
                    at = j * CHUNK + c * HD
                    v_ref[m, :, pl.ds(at, HD)] = conv(
                        m, pl.ds(CHUNK + at, HD), cv_ref, pl.ds(at, HD)
                    ).astype(BF16)

        def state_copy(h):
            return pltpu.make_async_remote_copy(
                src_ref=fwd_ref.at[h],
                dst_ref=got_ref.at[h],
                send_sem=st_send.at[h],
                recv_sem=st_recv.at[h],
                device_id={"ctx": ctx + 1},
                device_id_type=MESH,
            )

        def head_lanes(h):
            return pl.ds(pl.multiple_of(h * HD, HD), HD)

        def inside(m):
            return jnp.logical_and(starts[m] >= first, starts[m] < first + span)

        def states(h, carry):
            for m in range(windows):
                kept = jnp.logical_or(lane_pos >= starts[m], jnp.logical_not(inside(m)))
                feats = jnp.where(kept, features(kt_ref, (m, h)), 0.0).astype(BF16)
                state = jnp.dot(feats, v_ref[m, :, head_lanes(h)], preferred_element_type=F32)
                bs_ref[h, m] = state

                @pl.when(ctx == 0)
                def _():
                    fwd_ref[h, m] = state.astype(BF16)

            @pl.when(jnp.logical_and(ctx == 0, ctx_n > 1))
            def _():
                state_copy(h).start()

            return carry

        lax.fori_loop(0, heads, states, 0)

        row_pos = lax.broadcasted_iota(jnp.int32, (span, span), 0)
        other_pos = lax.broadcasted_iota(jnp.int32, (span, span), 1)
        lane_head = (lax.broadcasted_iota(jnp.int32, (1, 3 * HD), 1) % HD) // FD
        lag = hop_lag * jnp.maximum(ctx - 1, 0)

        def step(i, carry):
            late = i - lag
            due = jnp.logical_and(late >= 0, late < heads)

            @pl.when(jnp.logical_and(due, ctx > 0))
            def _():
                state_copy(late).wait_recv()

                @pl.when(ctx < ctx_n - 1)
                def _():
                    for m in range(windows):
                        old = got_ref[late, m].astype(F32)
                        fwd_ref[late, m] = (bs_ref[late, m] + jnp.where(inside(m), 0.0, old)).astype(BF16)
                    state_copy(late).start()

            @pl.when(i < heads)
            def _():
                for m in range(windows):
                    mine = jnp.where(lane_head == i, q3_ref[m], jnp.zeros((), BF16))
                    s = lax.dot_general(
                        mine, k3_ref[m], (((1,), (1,)), ((), ())), preferred_element_type=F32
                    ) * (1.0 / math.sqrt(FD))
                    edge = starts[m] - first
                    allowed = jnp.logical_and(
                        other_pos <= row_pos, (other_pos >= edge) == (row_pos >= edge)
                    )
                    weight = jnp.where(allowed, 1.0 + s + 0.5 * s * s, 0.0).astype(BF16)
                    num_ref[m, :, head_lanes(i)] = jnp.dot(
                        weight, v_ref[m, :, head_lanes(i)], preferred_element_type=F32
                    )

            @pl.when(due)
            def _():
                @pl.when(ctx > 0)
                def _():
                    for m in range(windows):
                        feats = features(qt_ref, (m, late)).astype(BF16)
                        far = lax.dot_general(
                            feats, got_ref[late, m], (((0,), (0,)), ((), ())), preferred_element_type=F32
                        )
                        used = jnp.logical_or(col_pos < starts[m], starts[m] < first)
                        num_ref[m, :, head_lanes(late)] += jnp.where(used, far, 0.0)

                for m in range(windows):
                    num = num_ref[m, :, head_lanes(late)]
                    square = jnp.mean(num * num, axis=1, keepdims=True)
                    gain = vg_ref[:, head_lanes(late)].astype(F32)
                    mix_ref[pl.ds(m * span, span), head_lanes(late)] = (num * lax.rsqrt(square + EPS) * gain).astype(BF16)

            return carry

        lax.fori_loop(0, steps, step, 0)

        def part_copy(j):
            return pltpu.make_async_remote_copy(
                src_ref=part_ref.at[j],
                dst_ref=other_ref.at[j],
                send_sem=p_send.at[j],
                recv_sem=p_recv.at[j],
                device_id={"head": mate},
                device_id_type=MESH,
            )

        wo_load.wait()
        for j in range(vchunks):
            at = pl.ds(pl.multiple_of(mate * half + j * CHUNK, CHUNK), CHUNK)
            part_ref[j] = jnp.dot(mix_ref[...], wo_v[:, at], preferred_element_type=F32)
            part_copy(j).start()

        window_rows = span * ctx_n
        valid = jnp.concatenate(
            [
                jnp.where(
                    first + lax.broadcasted_iota(jnp.int32, (span, CHUNK), 0) < window_rows - pad_ref[m], 1.0, 0.0
                )
                for m in range(windows)
            ],
            axis=0,
        )
        for j in range(vchunks):
            at = pl.ds(pl.multiple_of(core * half + j * CHUNK, CHUNK), CHUNK)
            mine = jnp.dot(mix_ref[...], wo_v[:, at], preferred_element_type=F32)
            part_copy(j).wait_recv()
            update = (mine + other_ref[j]) * valid
            out_ref[:, cols(j)] = (x_ref[core, :, cols(j)].astype(F32) + update).astype(BF16)

            @pl.when(sec < sec_n - 1)
            def _():
                section_copy(j).start()

        for j in range(vchunks):
            mate_copy(j).wait_send()
            part_copy(j).wait_send()

            @pl.when(sec < sec_n - 1)
            def _():
                section_copy(j).wait_send()

        @pl.when(ctx < ctx_n - 1)
        def _():
            for j in range(vchunks + 1):
                halo_copy(j).wait_send()

            def sent(h, carry):
                state_copy(h).wait_send()
                return carry

            lax.fori_loop(0, heads, sent, 0)

    return kernel


def local(
    tokens, norm_gain, w_query, w_key, w_value, conv_query, conv_key, conv_value, value_gain, w_out, doc_start, pad_length
):
    windows, span, half = tokens.shape
    width = 2 * half
    rows_n = windows * span
    heads = half // HD
    vchunks = half // CHUNK
    sizes = (lax.axis_size("ctx"), lax.axis_size("section"), windows, span, width, conv_query.shape[1])
    vmem = pl.BlockSpec(memory_space=pltpu.VMEM)
    smem = pl.BlockSpec(memory_space=pltpu.SMEM)
    hbm = pl.BlockSpec(memory_space=pl.ANY)
    dma = pltpu.SemaphoreType.DMA
    out = pl.pallas_call(
        make_kernel(sizes),
        out_shape=jax.ShapeDtypeStruct((rows_n, half), BF16),
        in_specs=[smem, smem, vmem, vmem, hbm, hbm, hbm, vmem, vmem, vmem, vmem, hbm],
        out_specs=vmem,
        scratch_shapes=[
            pltpu.VMEM((width, half + CHUNK), BF16),
            pltpu.VMEM((half, width), BF16),
            pltpu.VMEM((2, rows_n, half), BF16),
            pltpu.VMEM((rows_n, width), BF16),
            pltpu.VMEM((windows, span + 8, half + CHUNK), F32),
            pltpu.VMEM((windows, span, 3 * HD), BF16),
            pltpu.VMEM((windows, span, 3 * HD), BF16),
            pltpu.VMEM((windows, heads, 2 * FD, span), F32),
            pltpu.VMEM((windows, heads, 2 * FD, span), F32),
            pltpu.VMEM((windows, span, half), BF16),
            pltpu.VMEM((heads, windows, FROWS, HD), F32),
            pltpu.VMEM((heads, windows, FROWS, HD), BF16),
            pltpu.VMEM((heads, windows, FROWS, HD), BF16),
            pltpu.VMEM((windows, span, half), F32),
            pltpu.VMEM((rows_n, half), BF16),
            pltpu.VMEM((vchunks, rows_n, CHUNK), F32),
            pltpu.VMEM((vchunks, rows_n, CHUNK), F32),
            dma((3 + vchunks,)),
            dma((vchunks,)),
            dma((vchunks,)),
            dma((vchunks,)),
            dma((vchunks,)),
            dma((vchunks + 1,)),
            dma((vchunks + 1,)),
            dma((heads,)),
            dma((heads,)),
            dma((vchunks,)),
            dma((vchunks,)),
        ],
        compiler_params=pltpu.CompilerParams(
            collective_id=0, has_side_effects=True, vmem_limit_bytes=48 * 1024 * 1024
        ),
        name="layers",
    )(
        doc_start, pad_length, tokens.reshape(rows_n, half), norm_gain, w_query, w_key, w_value,
        conv_query, conv_key, conv_value, value_gain, w_out,
    )
    return out.reshape(1, windows, span, half)


def solution(mesh):
    return jax.shard_map(
        local,
        mesh=mesh,
        in_specs=(
            P("groups", "ctx", "head"),
            P("section", None),
            P("section", None, "head"),
            P("section", None, "head"),
            P("section", None, "head"),
            P("section", None, "head"),
            P("section", None, "head"),
            P("section", None, "head"),
            P("section", "head"),
            P("section", "head", None),
            P("groups"),
            P("groups"),
        ),
        out_specs=P("section", "groups", "ctx", "head"),
        check_vma=False,
    )
```

time: 350 us -> 83.2 us (0.24)
  waiting for transfers between devices: 176 us -> 0 us
  Pallas kernels: 0 us -> 74.1 us
  other arithmetic: 46.8 us -> 0 us
  matrix products: 34.3 us -> 0 us
  between operations: 23 us -> 0.02 us
  local copies, waits for them, and re-layouts: 31.5 us -> 8.66 us
  blocking collectives: 20.3 us -> 0 us
  starting transfers between devices: 14.6 us -> 0 us
    all_gather x3 -> x0, waiting for transfers between devices: 138 us -> none  [entering(): pieces = jax.tree.map(lambda part: lax.all_gather(part, axis), value)]
    pallas_call x0 -> x1, Pallas kernels: none -> 74.1 us  [local(): pl.pallas_call(make_kernel(sizes), out_shape=jax.ShapeDtypeStruct((rows_n...]
    dot_general x24 -> x0, matrix products: 34.3 us -> none  [the longest x3 11.7 us: local(): jnp.dot(mixed_rows, w_out[0], preferred_element_type=jnp.float32)]
    reduce_scatter x3 -> x0, waiting for transfers between devices: 26.3 us -> none  [local(): lax.psum_scatter(projected, 'head', scatter_dimension=1, tiled=True)]
    convert_element_type x30 -> x0, other arithmetic: 16.9 us -> none  [the longest x12 7.44 us: short_conv(): keep_rows = (earlier_side == after_start).astype(jnp.float32)]
    ppermute x11 -> x0, starting transfers between devices: 14.4 us -> none  [passed_along(): return lax.ppermute(block, axis, route)]
    ppermute x11 -> x0, waiting for transfers between devices: 12 us -> none  [passed_along(): return lax.ppermute(block, axis, route)]
    unnamed x1 -> x0, blocking collectives: 11.9 us -> none
  transfers between devices with their start and end apart: 17 -> 0, of which waited for: 8 -> 0; matrix products, arithmetic and copies ran while one was open for 12% -> 0% of each run, Pallas kernels for 0% -> 0%
where the time goes in v1:
time: 83.2 us; the launch traced here: 82.8 us
  Pallas kernels  74.1 us (89%)
  local copies, waits for them, and re-layouts  8.66 us (10%)
    pallas_call x1, Pallas kernels, local(): pl.pallas_call(make_kernel(sizes), out_shape=jax.ShapeDtypeStruct((rows_n...  74.1 us
    unnamed x21, local copies, waits for them, and re-layouts  8.66 us

profile of v1, /device:TPU:27, one launch (start us, length us, event | category | flops | bytes accessed | tf_op | source)
XLA Modules:
  0.0 82.8 jit_solution(925749518096883237)
XLA Ops:
  0.0 0.0 copy-start
  0.0 1.0 %copy-done = bf16[2,128,1024]{2,1,0:T(8,128)(2,1)S(1)} copy-done((bf16[2,128,1024]{2,1,0:T(8,128)(2,1)S(1)}, bf16[2,128,1024]{2,1,0:T(8,128)(2,1)}, u32[]{:S(2)}) %copy-start) | copy-done | bytes 524312
  1.0 0.0 copy-start.1
  1.0 1.0 %copy-done.1 = bf16[1,2048,128]{2,1,0:T(8,128)(2,1)S(1)} copy-done((bf16[1,2048,128]{2,1,0:T(8,128)(2,1)S(1)}, bf16[1,2048,128]{2,1,0:T(8,128)(2,1)}, u32[]{:S(2)}) %copy-start.1) | copy-done | bytes 524312
  2.1 0.0 copy-start.2
  2.1 1.0 %copy-done.2 = bf16[1,2048,128]{2,1,0:T(8,128)(2,1)S(1)} copy-done((bf16[1,2048,128]{2,1,0:T(8,128)(2,1)S(1)}, bf16[1,2048,128]{2,1,0:T(8,128)(2,1)}, u32[]{:S(2)}) %copy-start.2) | copy-done | bytes 524312
  3.1 0.0 copy-start.3
  3.1 0.7 copy-done.3
  3.8 0.0 copy-start.4
  3.8 0.7 copy-done.4
  4.5 0.0 copy-start.5
  4.5 0.7 copy-done.5
  5.2 0.0 copy-start.6
  5.2 0.7 copy-done.6
  5.9 0.0 copy-start.7
  5.9 0.7 copy-done.7
  6.6 0.0 copy-start.8
  6.6 0.7 copy-done.8
  7.2 0.0 copy-start.9
  7.2 0.7 copy-done.9
  7.9 74.1 %layers.1 = bf16[256,1024]{1,0:T(8,128)(2,1)S(1)} custom-call(s32[2]{0:T(128)S(1)} %copy-done.8, s32[2]{0:T(128)S(1)} %copy-done.9, bf16[256,1024]{1,0:T(8,128)(2,1)S(1)} %bitcast.3, bf16[1,2048]{1,0:T(2,128)(2,1)S(1)} %copy-done.3, bf16[1,2048,128]{2,1,0:T(8,128)(2,1)S(1)} %copy-done.1, bf16[1,2048,128]{2,1,0:T(8,128)(2,1)S(1)} %copy-done.2, ...), custom_call_target="tpu_custom_call" | custom-call | tf_op jit(solution)/shard_map/layers/pallas_call | solution.py:389
  82.0 0.8 copy.14
Async XLA Ops:
  0.0 1.0 %copy-start = (bf16[2,128,1024]{2,1,0:T(8,128)(2,1)S(1)}, bf16[2,128,1024]{2,1,0:T(8,128)(2,1)}, u32[]{:S(2)}) copy-start(bf16[2,128,1024]{2,1,0:T(8,128)(2,1)} %param.12) | copy-start | bytes 1572868
  1.0 1.0 %copy-start.1 = (bf16[1,2048,128]{2,1,0:T(8,128)(2,1)S(1)}, bf16[1,2048,128]{2,1,0:T(8,128)(2,1)}, u32[]{:S(2)}) copy-start(bf16[1,2048,128]{2,1,0:T(8,128)(2,1)} %wq_ref.1) | copy-start | bytes 1572868
  2.1 1.0 %copy-start.2 = (bf16[1,2048,128]{2,1,0:T(8,128)(2,1)S(1)}, bf16[1,2048,128]{2,1,0:T(8,128)(2,1)}, u32[]{:S(2)}) copy-start(bf16[1,2048,128]{2,1,0:T(8,128)(2,1)} %wk_ref.1) | copy-start | bytes 1572868
  3.1 0.7 copy-start.3
  3.8 0.7 copy-start.4
  4.5 0.7 copy-start.5
  5.2 0.7 copy-start.6
  5.9 0.7 copy-start.7
  6.6 0.7 copy-start.8
  7.2 0.7 copy-start.9

commit v2 on v1

--- a/solution.py
+++ b/solution.py
@@ -35,12 +35,12 @@
     rows_n = windows * span
     heads = half // HD
     vchunks = half // CHUNK
-    hop_lag = 2
-    steps = heads + hop_lag * max(ctx_n - 2, 0)
+    pair = heads // vchunks
 
     def kernel(
-        start_ref, pad_ref, tok_ref, gain_ref, wq_ref, wk_ref, wv_ref, cq_ref, ck_ref, cv_ref, vg_ref, wo_ref,
+        start_in, pad_in, tok_in, gain_in, wq_ref, wk_ref, wv_ref, cq_in, ck_in, cv_in, vg_in, wo_ref,
         out_ref,
+        start_ref, pad_ref, gain_ref, cq_ref, ck_ref, cv_ref, vg_ref, small_sem,
         w_all, wo_v, x_ref, n_ref, pr_ref, q3_ref, k3_ref, qt_ref, kt_ref, v_ref, bs_ref, got_ref, fwd_ref,
         num_ref, mix_ref, part_ref, other_ref,
         w_sem, x_send, x_recv, sec_send, sec_recv, halo_send, halo_recv, st_send, st_recv, p_send, p_recv,
@@ -49,6 +49,29 @@
         sec = lax.axis_index("section")
         core = lax.axis_index("head")
         mate = 1 - core
+
+        tok_load = pltpu.make_async_copy(tok_in, x_ref.at[core], small_sem.at[0])
+
+        @pl.when(sec == 0)
+        def _():
+            tok_load.start()
+
+        small = [
+            pltpu.make_async_copy(source, target, small_sem.at[1 + i])
+            for i, (source, target) in enumerate(
+                (
+                    (gain_in, gain_ref),
+                    (start_in, start_ref),
+                    (pad_in, pad_ref),
+                    (cq_in, cq_ref),
+                    (ck_in, ck_ref),
+                    (cv_in, cv_ref),
+                    (vg_in, vg_ref),
+                )
+            )
+        ]
+        for load in small:
+            load.start()
 
         loads = [
             pltpu.make_async_copy(wq_ref.at[0], w_all.at[:, pl.ds(0, HD)], w_sem.at[0]),
@@ -120,7 +143,7 @@
 
         @pl.when(sec == 0)
         def _():
-            x_ref[core] = tok_ref[...]
+            tok_load.wait()
 
         for j in range(vchunks):
 
@@ -129,6 +152,9 @@
                 section_copy(j).wait_recv()
 
             mate_copy(j).start()
+
+        for load in small:
+            load.wait()
 
         first = ctx * span
         col_pos = first + lax.broadcasted_iota(jnp.int32, (span, HD), 0)
@@ -165,20 +191,6 @@
         @pl.when(ctx == 0)
         def _():
             pr_ref[:, pl.ds(0, 8), :] = jnp.zeros((windows, 8, half + CHUNK), F32)
-
-        for j in range(vchunks + 1):
-            if j == 0:
-                loads[0].wait()
-                loads[1].wait()
-            else:
-                loads[1 + j].wait()
-            got = jnp.dot(n_ref[...], w_all[:, cols(j)], preferred_element_type=F32).astype(BF16).astype(F32)
-            for m in range(windows):
-                pr_ref[m, pl.ds(8, span), cols(j)] = got[m * span : (m + 1) * span]
-
-            @pl.when(ctx < ctx_n - 1)
-            def _():
-                halo_copy(j).start()
 
         def conv(m, at, taps_ref, tap_at):
             after = col_pos >= starts[m]
@@ -197,29 +209,42 @@
             def _():
                 halo_copy(j).wait_recv()
 
-        halo_wait(0)
-        for m in range(windows):
-            for which, taps_ref, wide_ref, turned_ref in ((0, cq_ref, q3_ref, qt_ref), (1, ck_ref, k3_ref, kt_ref)):
-                part = conv(m, pl.ds(which * HD, HD), taps_ref, pl.ds(0, HD))
-                high = part.astype(BF16)
-                low = (part - high.astype(F32)).astype(BF16)
-                wide_ref[m, :, pl.ds(0, HD)] = high
-                wide_ref[m, :, pl.ds(HD, HD)] = high if which == 0 else low
-                wide_ref[m, :, pl.ds(2 * HD, HD)] = low if which == 0 else high
-                turned = jnp.transpose(part)
-                for h in range(heads):
-                    own = turned[h * FD : (h + 1) * FD]
-                    turned_ref[m, h, pl.ds(0, FD), :] = own
-                    turned_ref[m, h, pl.ds(FD, FD), :] = own
-
-        for j in range(vchunks):
+        def project(j):
+            if j == 0:
+                loads[0].wait()
+                loads[1].wait()
+            else:
+                loads[1 + j].wait()
+            got = jnp.dot(n_ref[...], w_all[:, cols(j)], preferred_element_type=F32).astype(BF16).astype(F32)
+            for m in range(windows):
+                pr_ref[m, pl.ds(8, span), cols(j)] = got[m * span : (m + 1) * span]
+
+            @pl.when(ctx < ctx_n - 1)
+            def _():
+                halo_copy(j).start()
+
+        def conv_query_key():
+            halo_wait(0)
+            for m in range(windows):
+                for which, taps_ref, wide_ref, turned_ref in ((1, ck_ref, k3_ref, kt_ref), (0, cq_ref, q3_ref, qt_ref)):
+                    part = conv(m, pl.ds(which * HD, HD), taps_ref, pl.ds(0, HD))
+                    high = part.astype(BF16)
+                    low = (part - high.astype(F32)).astype(BF16)
+                    wide_ref[m, :, pl.ds(0, HD)] = high
+                    wide_ref[m, :, pl.ds(HD, HD)] = high if which == 0 else low
+                    wide_ref[m, :, pl.ds(2 * HD, HD)] = low if which == 0 else high
+                    turned = jnp.transpose(part)
+                    for h in range(heads):
+                        own = turned[h * FD : (h + 1) * FD]
+                        turned_ref[m, h, pl.ds(0, FD), :] = own
+                        turned_ref[m, h, pl.ds(FD, FD), :] = own
+
+        def conv_values(j):
             halo_wait(1 + j)
             for m in range(windows):
                 for c in range(CHUNK // HD):
                     at = j * CHUNK + c * HD
-                    v_ref[m, :, pl.ds(at, HD)] = conv(
-                        m, pl.ds(CHUNK + at, HD), cv_ref, pl.ds(at, HD)
-                    ).astype(BF16)
+                    v_ref[m, :, pl.ds(at, HD)] = conv(m, pl.ds(CHUNK + at, HD), cv_ref, pl.ds(at, HD)).astype(BF16)
 
         def state_copy(h):
             return pltpu.make_async_remote_copy(
@@ -237,82 +262,107 @@
         def inside(m):
             return jnp.logical_and(starts[m] >= first, starts[m] < first + span)
 
-        def states(h, carry):
-            for m in range(windows):
-                kept = jnp.logical_or(lane_pos >= starts[m], jnp.logical_not(inside(m)))
-                feats = jnp.where(kept, features(kt_ref, (m, h)), 0.0).astype(BF16)
-                state = jnp.dot(feats, v_ref[m, :, head_lanes(h)], preferred_element_type=F32)
-                bs_ref[h, m] = state
+        def states(p):
+            for h in range(p * pair, (p + 1) * pair):
+                made = []
+                for m in range(windows):
+                    kept = jnp.logical_or(lane_pos >= starts[m], jnp.logical_not(inside(m)))
+                    feats = jnp.where(kept, features(kt_ref, (m, h)), 0.0).astype(BF16)
+                    made.append(jnp.dot(feats, v_ref[m, :, pl.ds(h * HD, HD)], preferred_element_type=F32))
 
                 @pl.when(ctx == 0)
                 def _():
-                    fwd_ref[h, m] = state.astype(BF16)
-
-            @pl.when(jnp.logical_and(ctx == 0, ctx_n > 1))
-            def _():
-                state_copy(h).start()
-
-            return carry
-
-        lax.fori_loop(0, heads, states, 0)
+                    for m in range(windows):
+                        fwd_ref[h, m] = made[m].astype(BF16)
+                    if ctx_n > 1:
+                        state_copy(h).start()
+
+                @pl.when(ctx > 0)
+                def _():
+                    for m in range(windows):
+                        bs_ref[h, m] = made[m]
+
+        def pass_on(t):
+            p = t - 2 - ctx
+            due = jnp.logical_and(p >= 0, p < vchunks)
+            middle = jnp.logical_and(ctx > 0, ctx < ctx_n - 1)
+
+            @pl.when(jnp.logical_and(due, middle))
+            def _():
+                def one(i, carry):
+                    h = p * pair + i
+                    state_copy(h).wait_recv()
+                    for m in range(windows):
+                        old = got_ref[h, m].astype(F32)
+                        fwd_ref[h, m] = (bs_ref[h, m] + jnp.where(inside(m), 0.0, old)).astype(BF16)
+                    state_copy(h).start()
+                    return carry
+
+                lax.fori_loop(0, pair, one, 0)
+
+        project(0)
+        for t in range(1, vchunks + 2):
+            if t <= vchunks:
+                project(t)
+            if t == 1:
+                conv_query_key()
+            else:
+                conv_values(t - 2)
+                states(t - 2)
+            if t >= 3:
+                pass_on(t)
 
         row_pos = lax.broadcasted_iota(jnp.int32, (span, span), 0)
         other_pos = lax.broadcasted_iota(jnp.int32, (span, span), 1)
         lane_head = (lax.broadcasted_iota(jnp.int32, (1, 3 * HD), 1) % HD) // FD
-        lag = hop_lag * jnp.maximum(ctx - 1, 0)
-
-        def step(i, carry):
-            late = i - lag
-            due = jnp.logical_and(late >= 0, late < heads)
-
-            @pl.when(jnp.logical_and(due, ctx > 0))
-            def _():
-                state_copy(late).wait_recv()
-
-                @pl.when(ctx < ctx_n - 1)
+        local_steps = max(vchunks, ctx_n - 2)
+
+        def local_part(lp, carry):
+            pass_on(vchunks + 2 + lp)
+
+            @pl.when(lp < vchunks)
+            def _():
+                for c in range(pair):
+                    h = lp * pair + c
+                    for m in range(windows):
+                        mine = jnp.where(lane_head == h, q3_ref[m], jnp.zeros((), BF16))
+                        s = lax.dot_general(
+                            mine, k3_ref[m], (((1,), (1,)), ((), ())), preferred_element_type=F32
+                        ) * (1.0 / math.sqrt(FD))
+                        edge = starts[m] - first
+                        allowed = jnp.logical_and(other_pos <= row_pos, (other_pos >= edge) == (row_pos >= edge))
+                        weight = jnp.where(allowed, 1.0 + s + 0.5 * s * s, 0.0).astype(BF16)
+                        num_ref[m, :, head_lanes(h)] = jnp.dot(
+                            weight, v_ref[m, :, head_lanes(h)], preferred_element_type=F32
+                        )
+
+            return carry
+
+        lax.fori_loop(0, local_steps, local_part, 0)
+
+        def finish(h, carry):
+            @pl.when(ctx > 0)
+            def _():
+                @pl.when(ctx == ctx_n - 1)
                 def _():
-                    for m in range(windows):
-                        old = got_ref[late, m].astype(F32)
-                        fwd_ref[late, m] = (bs_ref[late, m] + jnp.where(inside(m), 0.0, old)).astype(BF16)
-                    state_copy(late).start()
-
-            @pl.when(i < heads)
-            def _():
+                    state_copy(h).wait_recv()
+
                 for m in range(windows):
-                    mine = jnp.where(lane_head == i, q3_ref[m], jnp.zeros((), BF16))
-                    s = lax.dot_general(
-                        mine, k3_ref[m], (((1,), (1,)), ((), ())), preferred_element_type=F32
-                    ) * (1.0 / math.sqrt(FD))
-                    edge = starts[m] - first
-                    allowed = jnp.logical_and(
-                        other_pos <= row_pos, (other_pos >= edge) == (row_pos >= edge)
+                    feats = features(qt_ref, (m, h)).astype(BF16)
+                    far = lax.dot_general(
+                        feats, got_ref[h, m], (((0,), (0,)), ((), ())), preferred_element_type=F32
                     )
-                    weight = jnp.where(allowed, 1.0 + s + 0.5 * s * s, 0.0).astype(BF16)
-                    num_ref[m, :, head_lanes(i)] = jnp.dot(
-                        weight, v_ref[m, :, head_lanes(i)], preferred_element_type=F32
-                    )
-
-            @pl.when(due)
-            def _():
-                @pl.when(ctx > 0)
-                def _():
-                    for m in range(windows):
-                        feats = features(qt_ref, (m, late)).astype(BF16)
-                        far = lax.dot_general(
-                            feats, got_ref[late, m], (((0,), (0,)), ((), ())), preferred_element_type=F32
-                        )
-                        used = jnp.logical_or(col_pos < starts[m], starts[m] < first)
-                        num_ref[m, :, head_lanes(late)] += jnp.where(used, far, 0.0)
-
-                for m in range(windows):
-                    num = num_ref[m, :, head_lanes(late)]
-                    square = jnp.mean(num * num, axis=1, keepdims=True)
-                    gain = vg_ref[:, head_lanes(late)].astype(F32)
-                    mix_ref[pl.ds(m * span, span), head_lanes(late)] = (num * lax.rsqrt(square + EPS) * gain).astype(BF16)
-
+                    used = jnp.logical_or(col_pos < starts[m], starts[m] < first)
+                    num_ref[m, :, head_lanes(h)] += jnp.where(used, far, 0.0)
+
+            for m in range(windows):
+                num = num_ref[m, :, head_lanes(h)]
+                square = jnp.mean(num * num, axis=1, keepdims=True)
+                gain = vg_ref[:, head_lanes(h)].astype(F32)
+                mix_ref[pl.ds(m * span, span), head_lanes(h)] = (num * lax.rsqrt(square + EPS) * gain).astype(BF16)
             return carry
 
-        lax.fori_loop(0, steps, step, 0)
+        lax.fori_loop(0, heads, finish, 0)
 
         def part_copy(j):
             return pltpu.make_async_remote_copy(
@@ -383,15 +433,22 @@
     vchunks = half // CHUNK
     sizes = (lax.axis_size("ctx"), lax.axis_size("section"), windows, span, width, conv_query.shape[1])
     vmem = pl.BlockSpec(memory_space=pltpu.VMEM)
-    smem = pl.BlockSpec(memory_space=pltpu.SMEM)
-    hbm = pl.BlockSpec(memory_space=pl.ANY)
+    hbm = pl.BlockSpec(memory_space=pltpu.MemorySpace.HBM)
     dma = pltpu.SemaphoreType.DMA
     out = pl.pallas_call(
         make_kernel(sizes),
         out_shape=jax.ShapeDtypeStruct((rows_n, half), BF16),
-        in_specs=[smem, smem, vmem, vmem, hbm, hbm, hbm, vmem, vmem, vmem, vmem, hbm],
+        in_specs=[hbm] * 12,
         out_specs=vmem,
         scratch_shapes=[
+            pltpu.SMEM((windows,), jnp.int32),
+            pltpu.SMEM((windows,), jnp.int32),
+            pltpu.VMEM(norm_gain.shape, BF16),
+            pltpu.VMEM(conv_query.shape, BF16),
+            pltpu.VMEM(conv_key.shape, BF16),
+            pltpu.VMEM(conv_value.shape, BF16),
+            pltpu.VMEM(value_gain.shape, BF16),
+            dma((8,)),
             pltpu.VMEM((width, half + CHUNK), BF16),
             pltpu.VMEM((half, width), BF16),
             pltpu.VMEM((2, rows_n, half), BF16),
@@ -422,7 +479,7 @@
             dma((vchunks,)),
         ],
         compiler_params=pltpu.CompilerParams(
-            collective_id=0, has_side_effects=True, vmem_limit_bytes=48 * 1024 * 1024
+            collective_id=0, has_side_effects=True, vmem_limit_bytes=60 * 1024 * 1024
         ),
         name="layers",
     )(

time: 83.2 us -> 78.5 us (0.944)
  local copies, waits for them, and re-layouts: 8.66 us -> 1.87 us
  Pallas kernels: 74.1 us -> 75.4 us
    unnamed x21 -> x1, local copies, waits for them, and re-layouts: 8.66 us -> 1.87 us
    pallas_call x1, Pallas kernels: 74.1 us -> 75.4 us  [local(): pl.pallas_call(make_kernel(sizes), out_shape=jax.ShapeDtypeStruct((rows_n...]
where the time goes in v2:
time: 78.5 us; the launch traced here: 77.3 us
  Pallas kernels  75.4 us (96%)
  local copies, waits for them, and re-layouts  1.87 us (2%)
    pallas_call x1, Pallas kernels, local(): pl.pallas_call(make_kernel(sizes), out_shape=jax.ShapeDtypeStruct((rows_n...  75.4 us
    unnamed x1, local copies, waits for them, and re-layouts  1.87 us

profile of v2, /device:TPU:27, one launch (start us, length us, event | category | flops | bytes accessed | tf_op | source)
XLA Modules:
  0.0 77.3 jit_solution(3546023660533317510)
XLA Ops:
  0.0 75.4 %layers.1 = bf16[256,1024]{1,0:T(8,128)(2,1)} custom-call(s32[2]{0:T(128)} %start_in.1, s32[2]{0:T(128)} %pad_in.1, bf16[256,1024]{1,0:T(8,128)(2,1)} %bitcast.3, bf16[1,2048]{1,0:T(2,128)(2,1)} %gain_in.1, bf16[1,2048,128]{2,1,0:T(8,128)(2,1)} %wq_ref.1, bf16[1,2048,128]{2,1,0:T(8,128)(2,1)} %wk_ref.1, bf16[1,2048,1024]{2,1,0:T(8,128)(2,1)} %wv_ref.1, ...), custom_call_target="tpu_custom_call" | custom-call | tf_op jit(solution)/shard_map/layers/pallas_call | solution.py:438
  75.4 1.9 %copy.14 = bf16[1,2,128,1024]{3,2,1,0:T(8,128)(2,1)} copy(bf16[1,2,128,1024]{3,2,1,0:T(8,128)(2,1)} %bitcast.2) | data formatting | bytes 1048576

commit v3 on v2

--- a/solution.py
+++ b/solution.py
@@ -36,13 +36,14 @@
     heads = half // HD
     vchunks = half // CHUNK
     pair = heads // vchunks
+    relay = sec_n % 2 == 0 and ctx_n > 1 and pair % 2 == 0
 
     def kernel(
         start_in, pad_in, tok_in, gain_in, wq_ref, wk_ref, wv_ref, cq_in, ck_in, cv_in, vg_in, wo_ref,
         out_ref,
         start_ref, pad_ref, gain_ref, cq_ref, ck_ref, cv_ref, vg_ref, small_sem,
         w_all, wo_v, x_ref, n_ref, pr_ref, q3_ref, k3_ref, qt_ref, kt_ref, v_ref, bs_ref, got_ref, fwd_ref,
-        num_ref, mix_ref, part_ref, other_ref,
+        num_ref, mix_ref, part_ref, other_ref, rel_ref, rel_send, rel_recv,
         w_sem, x_send, x_recv, sec_send, sec_recv, halo_send, halo_recv, st_send, st_recv, p_send, p_recv,
     ):
         ctx = lax.axis_index("ctx")
@@ -116,7 +117,57 @@
             + jnp.where(sec > 0, 1, 0)
             + jnp.where(sec < sec_n - 1, 1, 0)
         )
+        across = sec + 1 - 2 * (sec % 2)
+        if relay:
+
+            @pl.when(ctx > 0)
+            def _():
+                pl.semaphore_signal(
+                    barrier, inc=1, device_id={"ctx": ctx - 1, "section": across}, device_id_type=MESH
+                )
+
+            @pl.when(ctx < ctx_n - 1)
+            def _():
+                pl.semaphore_signal(
+                    barrier, inc=1, device_id={"ctx": ctx + 1, "section": across}, device_id_type=MESH
+                )
+
+            peers = peers + jnp.where(ctx > 0, 1, 0) + jnp.where(ctx < ctx_n - 1, 1, 0)
         pl.semaphore_wait(barrier, peers)
+
+        def relay_copy(r):
+            return pltpu.make_async_remote_copy(
+                src_ref=rel_ref.at[r],
+                dst_ref=got_ref.at[2 * r],
+                send_sem=rel_send.at[r],
+                recv_sem=st_recv.at[2 * r],
+                device_id={"section": across},
+                device_id_type=MESH,
+            )
+
+        def detour_copy(r):
+            return pltpu.make_async_remote_copy(
+                src_ref=fwd_ref.at[2 * r],
+                dst_ref=rel_ref.at[r],
+                send_sem=st_send.at[2 * r],
+                recv_sem=rel_recv.at[r],
+                device_id={"ctx": ctx + 1, "section": across},
+                device_id_type=MESH,
+            )
+
+        def relay_all(parity):
+            if relay:
+
+                @pl.when(jnp.logical_and(sec % 2 == parity, ctx > 0))
+                def _():
+                    def one(r, carry):
+                        detour_copy(r).wait_recv()
+                        relay_copy(r).start()
+                        return carry
+
+                    lax.fori_loop(0, heads // 2, one, 0)
+
+        relay_all(1)
 
         def cols(j):
             return pl.ds(j * CHUNK, CHUNK)
@@ -256,6 +307,12 @@
                 device_id_type=MESH,
             )
 
+        def state_start(r, odd):
+            if relay and odd == 0:
+                detour_copy(r).start()
+            else:
+                state_copy(2 * r + odd).start()
+
         def head_lanes(h):
             return pl.ds(pl.multiple_of(h * HD, HD), HD)
 
@@ -275,7 +332,7 @@
                     for m in range(windows):
                         fwd_ref[h, m] = made[m].astype(BF16)
                     if ctx_n > 1:
-                        state_copy(h).start()
+                        state_start(h // 2, h % 2)
 
                 @pl.when(ctx > 0)
                 def _():
@@ -295,10 +352,11 @@
                     for m in range(windows):
                         old = got_ref[h, m].astype(F32)
                         fwd_ref[h, m] = (bs_ref[h, m] + jnp.where(inside(m), 0.0, old)).astype(BF16)
-                    state_copy(h).start()
+                    state_start(p * (pair // 2) + i // 2, i % 2)
                     return carry
 
-                lax.fori_loop(0, pair, one, 0)
+                for i in range(pair):
+                    one(i, 0)
 
         project(0)
         for t in range(1, vchunks + 2):
@@ -400,6 +458,18 @@
             @pl.when(sec < sec_n - 1)
             def _():
                 section_copy(j).start()
+
+        relay_all(0)
+
+        if relay:
+
+            @pl.when(ctx > 0)
+            def _():
+                def relayed(r, carry):
+                    relay_copy(r).wait_send()
+                    return carry
+
+                lax.fori_loop(0, heads // 2, relayed, 0)
 
         for j in range(vchunks):
             mate_copy(j).wait_send()
@@ -466,6 +536,9 @@
             pltpu.VMEM((rows_n, half), BF16),
             pltpu.VMEM((vchunks, rows_n, CHUNK), F32),
             pltpu.VMEM((vchunks, rows_n, CHUNK), F32),
+            pltpu.VMEM((heads // 2, windows, FROWS, HD), BF16),
+            dma((heads // 2,)),
+            dma((heads // 2,)),
             dma((3 + vchunks,)),
             dma((vchunks,)),
             dma((vchunks,)),

time: 78.5 us -> 88.1 us (1.12); the launches traced: 77.3 us -> 87.9 us
  Pallas kernels: 75.4 us -> 86.1 us
    pallas_call x1, Pallas kernels: 75.4 us -> 86.1 us  [local(): pl.pallas_call(make_kernel(sizes), out_shape=jax.ShapeDtypeStruct((rows_n...]
where the time goes in v3:
time: 88.1 us; the launch traced here: 87.9 us
  Pallas kernels  86.1 us (98%)
  local copies, waits for them, and re-layouts  1.87 us (2%)
    pallas_call x1, Pallas kernels, local(): pl.pallas_call(make_kernel(sizes), out_shape=jax.ShapeDtypeStruct((rows_n...  86.1 us
    unnamed x1, local copies, waits for them, and re-layouts  1.87 us

profile of v3, /device:TPU:27, one launch (start us, length us, event | category | flops | bytes accessed | tf_op | source)
XLA Modules:
  0.0 87.9 jit_solution(4664914919791049373)
XLA Ops:
  0.0 86.1 %layers.1 = bf16[256,1024]{1,0:T(8,128)(2,1)} custom-call(s32[2]{0:T(128)} %start_in.1, s32[2]{0:T(128)} %pad_in.1, bf16[256,1024]{1,0:T(8,128)(2,1)} %bitcast.3, bf16[1,2048]{1,0:T(2,128)(2,1)} %gain_in.1, bf16[1,2048,128]{2,1,0:T(8,128)(2,1)} %wq_ref.1, bf16[1,2048,128]{2,1,0:T(8,128)(2,1)} %wk_ref.1, bf16[1,2048,1024]{2,1,0:T(8,128)(2,1)} %wv_ref.1, ...), custom_call_target="tpu_custom_call" | custom-call | tf_op jit(solution)/shard_map/layers/pallas_call | solution.py:508
  86.1 1.9 %copy.14 = bf16[1,2,128,1024]{3,2,1,0:T(8,128)(2,1)} copy(bf16[1,2,128,1024]{3,2,1,0:T(8,128)(2,1)} %bitcast.2) | data formatting | bytes 1048576
